TPU v7x, 256 devices: a whole 4x4x8 slice. The times are simulated.
256 devices in a mesh: expert: 64 (over z, y, core), tensor: 4 (over x).
Axes of the slice: x: 4, y: 4, z: 8, core: 2. Of those that a mesh axis runs over, the one named last changes fastest.
Arguments:
- context: bfloat16 [8192, 4096], P('expert', 'tensor'), may hold values from -6 to 6
- residual_in: bfloat16 [8192, 4096], P('expert')
- out_weight: bfloat16 [4096, 4096], P('tensor', 'expert'), may hold values from -0.09375 to 0.09375
- norm_gain: bfloat16 [4096], replicated, may hold values from 0.099609375 to 1.8984375
- expert_ids: int32 [8192, 8], P('expert'), may hold values from 0 to 63, all different within a row; in each aligned block of 128 rows (0 to 127, 128 to 255, ...) at most 18 rows name the same one
- gate_weights: float32 [8192, 8], P('expert'), may hold values from 0.1 to 1
- gate_matrix: bfloat16 [64, 4096, 1536], P('expert', None, 'tensor'), may hold values from -0.09375 to 0.09375
- lift_matrix: bfloat16 [64, 4096, 1536], P('expert', None, 'tensor'), may hold values from -0.09375 to 0.09375
- down_matrix: bfloat16 [64, 1536, 4096], P('expert', 'tensor'), may hold values from -0.15625 to 0.15625
Outputs:
- layer_out: bfloat16 [8192, 4096], P('expert', 'tensor')
Inputs may be any that keep to these rules, and one draw needn't show every extreme that they name: `expert_ids`: each row names 8 different experts. Within each aligned block of 128 rows (the rows of one index of the expert axis) no expert is named more than 18 times, a bound that some block reaches.
All inputs are finite; a program needn't handle non-finite values.
Results may differ from a plain program's by a relative error of at most 0.009.
Values may be sent and summed in bfloat16 or wider, within the bound.
No kernel may reach another device: no remote copies, remote signals or barrier semaphores. Data moves between devices by JAX's collectives and lax.ppermute only.
A program may use at most 128 MiB of HBM per device.

v0:
```python
import jax
import jax.numpy as jnp
from jax import lax
from jax.sharding import PartitionSpec as P

epsilon = 1e-06


def body(
    context,
    residual_in,
    out_weight,
    norm_gain,
    expert_ids,
    gate_weights,
    gate_matrix,
    lift_matrix,
    down_matrix,
):
    tokens_here, model_width = residual_in.shape
    top_count = expert_ids.shape[1]
    share_width = model_width // lax.axis_size("tensor")
    column_start = lax.axis_index("tensor") * share_width
    experts_all = lax.axis_size("expert") * gate_matrix.shape[0]
    capacity = min(tokens_here, max(2, tokens_here * top_count * 9 // (8 * experts_all)))
    attention_part = jnp.dot(
        context,
        lax.all_gather(out_weight, "expert", axis=1, tiled=True),
        preferred_element_type=jnp.float32,
    )
    attention_out = lax.psum(attention_part, "tensor")
    hidden_state = (residual_in.astype(jnp.float32) + attention_out).astype(jnp.bfloat16)
    widened = hidden_state.astype(jnp.float32)
    squares_mean = jnp.mean(widened * widened, axis=1, keepdims=True)
    normed_full = (
        widened * lax.rsqrt(squares_mean + epsilon) * norm_gain.astype(jnp.float32)
    ).astype(jnp.bfloat16)
    hidden_share = lax.dynamic_slice_in_dim(hidden_state, column_start, share_width, 1)
    flat_ids = expert_ids.reshape(-1)
    onehot_table = (flat_ids[:, None] == jnp.arange(experts_all, dtype=jnp.int32)[None, :]).astype(
        jnp.int32
    )
    earlier = jnp.cumsum(onehot_table, axis=0) - onehot_table
    slot_index = jnp.sum(earlier * onehot_table, axis=1)
    destination = flat_ids * capacity + slot_index
    token_index = jnp.arange(tokens_here * top_count, dtype=jnp.int32) // top_count
    source_width = normed_full.shape[1]
    buffer_rows = jnp.zeros((experts_all * capacity, source_width), jnp.bfloat16)
    buffer_rows = buffer_rows.at[destination].set(normed_full[token_index])
    buffer_rows = buffer_rows.reshape(experts_all, capacity, source_width)
    received = lax.all_to_all(buffer_rows, "expert", split_axis=0, concat_axis=0, tiled=True)
    senders = received.shape[0]
    slots_here = received.shape[1]
    flat_rows = received.reshape(senders * slots_here, model_width)
    gate_values = jnp.dot(flat_rows, gate_matrix[0], preferred_element_type=jnp.float32)
    lift_values = jnp.dot(flat_rows, lift_matrix[0], preferred_element_type=jnp.float32)
    activation = (jax.nn.silu(gate_values) * lift_values).astype(jnp.bfloat16)
    partial_out = jnp.dot(activation, down_matrix[0], preferred_element_type=jnp.float32)
    expert_partial = partial_out.reshape(senders, slots_here, model_width)
    expert_share = lax.psum_scatter(
        expert_partial.astype(jnp.bfloat16), "tensor", scatter_dimension=2, tiled=True
    )
    returned = lax.all_to_all(expert_share, "expert", split_axis=0, concat_axis=0, tiled=True)
    picked = returned.reshape(experts_all * capacity, share_width)[destination]
    picked = picked.reshape(tokens_here, top_count, share_width)
    moe_share = jnp.sum(gate_weights[:, :, None] * picked.astype(jnp.float32), axis=1)
    return (hidden_share.astype(jnp.float32) + moe_share).astype(jnp.bfloat16)


def solution(mesh):
    placed = (
        P("expert", "tensor"),
        P("expert", None),
        P("tensor", "expert"),
        P(),
        P("expert", None),
        P("expert", None),
        P("expert", None, "tensor"),
        P("expert", None, "tensor"),
        P("expert", "tensor", None),
    )
    return jax.shard_map(
        body, mesh=mesh, in_specs=placed, out_specs=P("expert", "tensor"), check_vma=False
    )
```

profile of v0, /device:TPU:8, one launch (start us, length us, event | category | flops | bytes accessed | tf_op | source)
XLA Modules:
  0.0 744.2 jit_solution(13246930377981361659)
XLA Ops:
  7.3 87.5 %all-gather.2.cloned.1.call-done = bf16[1024,4096]{0,1:T(8,128)(2,1)} async-done(((bf16[1024,64]{0,1:T(8,128)(2,1)}), bf16[1024,4096]{0,1:T(8,128)(2,1)}) %all-gather.2.cloned.1.call-update) | async-done | bytes 8388624 | tf_op jit(solution)/shard_map/all_gather | solution.py:28
  94.8 7.7 %fusion.18 = f32[128,4096]{1,0:T(8,128)} fusion(bf16[128,1024]{1,0:T(8,128)(2,1)} %param.9, bf16[1024,4096]{0,1:T(8,128)(2,1)} %all-gather.2.cloned.1.call-done), kind=kOutput, calls=%fused_computation.40 | convolution fusion | flops 1073741824 | bytes 10747904 | tf_op jit(solution)/shard_map/dot_general | solution.py:26
  103.6 31.1 %reduce-window.6 = s32[64,8,128]{2,1,0:T(8,128)S(1)} reduce-window(s32[64,8,128]{2,1,0:T(8,128)} %fusion.17, s32[]{:T(128)} %constant.17.clone.1), window={size=1x1x128 pad=0_0x0_0x127_0}, to_apply=%region_1.0 | reduce-window | flops 8323072 | bytes 524292 | tf_op jit(solution)/shard_map/reduce-window
  135.6 1.1 copy.24
  137.3 27.9 %all-reduce.2.cloned.1.call-done = f32[128,4096]{1,0:T(8,128)} async-done(((f32[128,4096]{1,0:T(8,128)}), f32[128,4096]{1,0:T(8,128)}) %all-reduce.2.cloned.1.call-update) | async-done | bytes 2097168 | tf_op jit(solution)/shard_map/psum | solution.py:31
  165.1 2.3 fusion.10
  168.5 1.4 fusion.12
  169.9 16.4 %gather_fusion = bf16[1024,4096]{1,0:T(8,128)(2,1)} fusion(bf16[128,4096]{1,0:T(8,128)(2,1)} %fusion.12, s32[1024]{0:T(1024)S(1)} %broadcast_clamp_fusion.1), kind=kCustom, calls=%fused_computation | custom fusion | bytes 16781312 | tf_op jit(solution)/shard_map/gather | solution.py:49
  186.3 18.2 %scatter_custom_fusion = bf16[1152,4096]{1,0:T(8,128)(2,1)} fusion(s32[1024]{0:T(1024)S(1)} %bitcast.43, bf16[1024,4096]{1,0:T(8,128)(2,1)} %gather_fusion, bf16[]{:T(256)} %constant.38.clone.1), kind=kCustom, calls=%fused_computation.4 | custom fusion | bytes 9437696 | tf_op jit(solution)/shard_map/scatter | solution.py:49
  204.5 13.9 %reshape.114 = bf16[64,18,4096]{2,1,0:T(8,128)(2,1)} reshape(bf16[1152,4096]{1,0:T(8,128)(2,1)} %scatter_custom_fusion) | data formatting | bytes 18874368 | tf_op jit(solution)/shard_map/reshape | solution.py:50
  218.4 286.6 %all_to_all.10 = bf16[64,18,4096]{2,1,0:T(8,128)(2,1)} all-to-all(bf16[64,18,4096]{2,1,0:T(8,128)(2,1)} %reshape.114), channel_id=1, replica_groups=mesh['expert'=64,'tensor'=4] {'expert'}, dimensions={0} | all-to-all | bytes 18874368 | tf_op jit(solution)/shard_map/all_to_all | solution.py:51
  505.0 14.2 %reshape.115 = bf16[1152,4096]{1,0:T(8,128)(2,1)} reshape(bf16[64,18,4096]{2,1,0:T(8,128)(2,1)} %all_to_all.10) | data formatting | bytes 18874368 | tf_op jit(solution)/shard_map/reshape | solution.py:54
  519.2 8.7 %fusion.5 = f32[1152,384]{1,0:T(8,128)S(1)} fusion(bf16[1152,4096]{1,0:T(8,128)(2,1)} %reshape.115, bf16[1,4096,384]{2,1,0:T(8,128)(2,1)} %param.15), kind=kOutput, calls=%fused_computation.11 | convolution fusion | flops 3623878656 | bytes 14352384 | tf_op jit(solution)/shard_map/dot_general | solution.py:55
  527.9 6.2 fusion.7
  534.1 2.2 dot_general.17
  536.3 8.7 %convolution_convert_fusion = bf16[64,18,4096]{2,0,1:T(8,128)(2,1)} fusion(bf16[1,384,4096]{2,1,0:T(8,128)(2,1)S(1)} %copy-done, bf16[64,18,384]{2,1,0:T(8,128)(2,1)} %dot_general.17), kind=kOutput, calls=%fused_computation.3 | convolution fusion | flops 3628597248 | bytes 13467648 | tf_op jit(solution)/shard_map/dot_general | solution.py:58
  545.0 86.4 %reduce-scatter.2.cloned.1.call-done = bf16[64,18,1024]{2,0,1:T(8,128)(2,1)} async-done(((bf16[64,18,4096]{2,0,1:T(8,128)(2,1)}), bf16[64,18,1024]{2,0,1:T(8,128)(2,1)}) %reduce-scatter.2.cloned.1.call-update) | async-done | bytes 2359312 | tf_op jit(solution)/shard_map/reduce_scatter | solution.py:60
  631.4 4.7 copy.27
  636.2 10.9 %all-to-all-start.1 = ((bf16[64,18,1024]{2,1,0:T(8,128)(2,1)}), bf16[64,18,1024]{2,1,0:T(8,128)(2,1)}, u32[]{:S(2)}, u32[]{:S(2)}) async-start(bf16[64,18,1024]{2,1,0:T(8,128)(2,1)} %copy.27), calls=%async_computation.2 | async-start | bytes 6291456 | tf_op jit(solution)/shard_map/all_to_all | solution.py:63
  647.2 73.5 %all-to-all-done.1 = bf16[64,18,1024]{2,1,0:T(8,128)(2,1)} async-done(((bf16[64,18,1024]{2,1,0:T(8,128)(2,1)}), bf16[64,18,1024]{2,1,0:T(8,128)(2,1)}, u32[]{:S(2)}, u32[]{:S(2)}) %all-to-all-start.1) | async-done | bytes 2359328 | tf_op jit(solution)/shard_map/all_to_all | solution.py:63
  720.7 4.3 reshape.116
  725.0 8.0 %gather_fusion.1 = bf16[1024,1024]{1,0:T(8,128)(2,1)} fusion(bf16[1152,1024]{1,0:T(8,128)(2,1)} %reshape.116, s32[1024]{0:T(1024)S(1)} %broadcast_clamp_fusion), kind=kCustom, calls=%fused_computation.1 | custom fusion | bytes 4198400 | tf_op jit(solution)/shard_map/gather | solution.py:64
  733.0 2.9 fusion.2
  735.9 1.7 add_convert_fusion.1
  (40 shorter events, 4.4 us)
Async XLA Ops:
  6.5 529.8 %copy-start = (bf16[1,384,4096]{2,1,0:T(8,128)(2,1)S(1)}, bf16[1,384,4096]{2,1,0:T(8,128)(2,1)}, u32[]{:S(2)}) copy-start(bf16[1,384,4096]{2,1,0:T(8,128)(2,1)} %param.17) | copy-start | bytes 9437188
  6.5 88.3 %all-gather.2.cloned.1.call-start = ((), (), s32[]{:S(2)}) async-start(), calls=%async_computation.3 | async-start | bytes 8519680 | tf_op jit(solution)/shard_map/all_gather | solution.py:28
  7.3 95.3 %copy-start.3 = (s32[128,8]{0,1:T(8,128)S(1)}, s32[128,8]{0,1:T(8,128)}, u32[]{:S(2)}) copy-start(s32[128,8]{0,1:T(8,128)} %param.13) | copy-start | bytes 12292
  7.3 157.9 %all-reduce.2.cloned.1.call-start = ((), (), s32[]{:S(2)}) async-start(), calls=%async_computation.4 | async-start | bytes 4194304 | tf_op jit(solution)/shard_map/psum | solution.py:31
  102.5 34.5 %copy-start.4 = (bf16[4096]{0:T(1024)(128)(2,1)S(1)}, bf16[4096]{0:T(1024)(128)(2,1)}, u32[]{:S(2)}) copy-start(bf16[4096]{0:T(1024)(128)(2,1)} %param.12) | copy-start | bytes 24580
  102.6 528.9 %reduce-scatter.2.cloned.1.call-start = ((), (), s32[]{:S(2)}) async-start(), calls=%async_computation.5 | async-start | bytes 11796480 | tf_op jit(solution)/shard_map/reduce_scatter | solution.py:60
  167.4 1.1 copy-start.2
  519.2 8.7 %copy-start.1 = (bf16[1152,4096]{1,0:T(8,128)(2,1)S(1)}, bf16[1152,4096]{1,0:T(8,128)(2,1)}, u32[]{:S(2)}) copy-start(bf16[1152,4096]{1,0:T(8,128)(2,1)} %reshape.115) | copy-start | bytes 28311556
  519.2 8.7 %copy-start.6 = (bf16[1,4096,384]{2,1,0:T(8,128)(2,1)S(1)}, bf16[1,4096,384]{2,1,0:T(8,128)(2,1)}, u32[]{:S(2)}) copy-start(bf16[1,4096,384]{2,1,0:T(8,128)(2,1)} %param.16) | copy-start | bytes 9437188
  636.2 10.9 %copy-start.5 = (f32[128,8]{0,1:T(8,128)S(1)}, f32[128,8]{0,1:T(8,128)}, u32[]{:S(2)}) copy-start(f32[128,8]{0,1:T(8,128)} %param.14) | copy-start | bytes 12292
  636.2 84.5 %all-to-all-start.1 = ((bf16[64,18,1024]{2,1,0:T(8,128)(2,1)}), bf16[64,18,1024]{2,1,0:T(8,128)(2,1)}, u32[]{:S(2)}, u32[]{:S(2)}) async-start(bf16[64,18,1024]{2,1,0:T(8,128)(2,1)} %copy.27), calls=%async_computation.2 | async-start | bytes 6291456 | tf_op jit(solution)/shard_map/all_to_all | solution.py:63
Sparse Core Ops, SparseCore 0:
  10.1 84.6 all-gather.1
  102.7 62.4 all-reduce.1
  545.1 86.2 reduce-scatter.1
where the time goes:
time: 747 us; the launch traced here: 744 us
  blocking collectives  287 us (38%)
  waiting for transfers between devices  276 us (37%)
  local copies, waits for them, and re-layouts  85.7 us (11%)
  other arithmetic  40.4 us (5%)
  matrix products  31.3 us (4%)
  between operations  13.3 us (2%)
  starting transfers between devices  11 us (1%)
    all_to_all x1, blocking collectives, body(): lax.all_to_all(buffer_rows, 'expert', split_axis=0, concat_axis=0, tiled=...  287 us
    all_gather x1, waiting for transfers between devices, body(): lax.all_gather(out_weight, 'expert', axis=1, tiled=True)  87.5 us
    reduce_scatter x1, waiting for transfers between devices, body(): lax.psum_scatter(expert_partial.astype(jnp.bfloat16), 'tensor', scatter_d...  86.4 us
    all_to_all x1, waiting for transfers between devices, body(): lax.all_to_all(expert_share, 'expert', split_axis=0, concat_axis=0, tiled...  73.5 us
    another operation x3, other arithmetic  31.3 us
    psum x1, waiting for transfers between devices, body(): attention_out = lax.psum(attention_part, 'tensor')  27.9 us
    scatter x1, local copies, waits for them, and re-layouts, body(): buffer_rows = buffer_rows.at[destination].set(normed_full[token_index])  18.2 us
    gather x1, local copies, waits for them, and re-layouts, body(): buffer_rows = buffer_rows.at[destination].set(normed_full[token_index])  16.4 us
  transfers between devices with their start and end apart: 4, of which 4 were waited for; matrix products, arithmetic and copies ran while one was open for 5% of the time, Pallas kernels for 0%

commit v1 on v0

--- a/solution.py
+++ b/solution.py
@@ -28,7 +28,7 @@
         lax.all_gather(out_weight, "expert", axis=1, tiled=True),
         preferred_element_type=jnp.float32,
     )
-    attention_out = lax.psum(attention_part, "tensor")
+    attention_out = jnp.sum(lax.all_gather(attention_part, "tensor"), axis=0)
     hidden_state = (residual_in.astype(jnp.float32) + attention_out).astype(jnp.bfloat16)
     widened = hidden_state.astype(jnp.float32)
     squares_mean = jnp.mean(widened * widened, axis=1, keepdims=True)

time: 747 us -> 775 us (1.037)
  waiting for transfers between devices: 276 us -> 299 us
    all_gather x0 -> x1, waiting for transfers between devices: none -> 49.6 us  [body(): attention_out = jnp.sum(lax.all_gather(attention_part, 'tensor'), axis=0)]
    psum x1 -> x0, waiting for transfers between devices: 27.9 us -> none  [body(): attention_out = lax.psum(attention_part, 'tensor')]
  transfers between devices with their start and end apart: 4 -> 4, of which waited for: 4 -> 4; matrix products, arithmetic and copies ran while one was open for 5% -> 4% of each run, Pallas kernels for 0% -> 0%
where the time goes in v1:
time: 775 us; the launch traced here: 773 us
  waiting for transfers between devices  299 us (39%)
  blocking collectives  287 us (37%)
  local copies, waits for them, and re-layouts  85.7 us (11%)
  other arithmetic  46 us (6%)
  matrix products  31.3 us (4%)
  between operations  13.3 us (2%)
  starting transfers between devices  11 us (1%)
    all_to_all x1, blocking collectives, body(): lax.all_to_all(buffer_rows, 'expert', split_axis=0, concat_axis=0, tiled=...  287 us
    reduce_scatter x1, waiting for transfers between devices, body(): lax.psum_scatter(expert_partial.astype(jnp.bfloat16), 'tensor', scatter_d...  87.5 us
    all_gather x1, waiting for transfers between devices, body(): lax.all_gather(out_weight, 'expert', axis=1, tiled=True)  87.5 us
    all_to_all x1, waiting for transfers between devices, body(): lax.all_to_all(expert_share, 'expert', split_axis=0, concat_axis=0, tiled...  73.5 us
    all_gather x1, waiting for transfers between devices, body(): attention_out = jnp.sum(lax.all_gather(attention_part, 'tensor'), axis=0)  49.6 us
    another operation x3, other arithmetic  31.3 us
    scatter x1, local copies, waits for them, and re-layouts, body(): buffer_rows = buffer_rows.at[destination].set(normed_full[token_index])  18.2 us
    gather x1, local copies, waits for them, and re-layouts, body(): buffer_rows = buffer_rows.at[destination].set(normed_full[token_index])  16.4 us
  transfers between devices with their start and end apart: 4, of which 4 were waited for; matrix products, arithmetic and copies ran while one was open for 4% of the time, Pallas kernels for 0%

profile of v1, /device:TPU:8, one launch (start us, length us, event | category | flops | bytes accessed | tf_op | source)
XLA Modules:
  0.0 772.8 jit_solution(17334947730129627819)
XLA Ops:
  7.3 87.5 %all-gather.4.cloned.1.call-done = bf16[1024,4096]{0,1:T(8,128)(2,1)} async-done(((bf16[1024,64]{0,1:T(8,128)(2,1)}), bf16[1024,4096]{0,1:T(8,128)(2,1)}) %all-gather.4.cloned.1.call-update) | async-done | bytes 8388624 | tf_op jit(solution)/shard_map/all_gather | solution.py:28
  94.8 7.7 fusion.18
  103.6 31.2 %reduce-window.6 = s32[64,8,128]{2,1,0:T(8,128)S(1)} reduce-window(s32[64,8,128]{2,1,0:T(8,128)} %fusion.17, s32[]{:T(128)} %constant.20.clone.1), window={size=1x1x128 pad=0_0x0_0x127_0}, to_apply=%region_1.0 | reduce-window | flops 8323072 | bytes 524292 | tf_op jit(solution)/shard_map/reduce-window
  137.3 49.6 %all-gather.6.cloned.1.call-done = f32[512,4096]{1,0:T(8,128)} async-done(((f32[128,4096]{1,0:T(8,128)}), f32[512,4096]{1,0:T(8,128)}) %all-gather.6.cloned.1.call-update) | async-done | bytes 8388624 | tf_op jit(solution)/shard_map/all_gather | solution.py:31
  187.0 5.6 reduce_sum.38
  192.5 2.3 fusion.10
  195.9 1.4 fusion.12
  197.3 16.4 %gather_fusion = bf16[1024,4096]{1,0:T(8,128)(2,1)} fusion(bf16[128,4096]{1,0:T(8,128)(2,1)} %fusion.12, s32[1024]{0:T(1024)S(1)} %broadcast_clamp_fusion.1), kind=kCustom, calls=%fused_computation | custom fusion | bytes 16781312 | tf_op jit(solution)/shard_map/gather | solution.py:49
  213.7 18.2 %scatter_custom_fusion = bf16[1152,4096]{1,0:T(8,128)(2,1)} fusion(s32[1024]{0:T(1024)S(1)} %bitcast.45, bf16[1024,4096]{1,0:T(8,128)(2,1)} %gather_fusion, bf16[]{:T(256)} %constant.39.clone.1), kind=kCustom, calls=%fused_computation.4 | custom fusion | bytes 9437696 | tf_op jit(solution)/shard_map/scatter | solution.py:49
  231.9 13.9 %reshape.114 = bf16[64,18,4096]{2,1,0:T(8,128)(2,1)} reshape(bf16[1152,4096]{1,0:T(8,128)(2,1)} %scatter_custom_fusion) | data formatting | bytes 18874368 | tf_op jit(solution)/shard_map/reshape | solution.py:50
  245.8 286.7 %all_to_all.10 = bf16[64,18,4096]{2,1,0:T(8,128)(2,1)} all-to-all(bf16[64,18,4096]{2,1,0:T(8,128)(2,1)} %reshape.114), channel_id=1, replica_groups=mesh['expert'=64,'tensor'=4] {'expert'}, dimensions={0} | all-to-all | bytes 18874368 | tf_op jit(solution)/shard_map/all_to_all | solution.py:51
  532.4 14.2 %reshape.115 = bf16[1152,4096]{1,0:T(8,128)(2,1)} reshape(bf16[64,18,4096]{2,1,0:T(8,128)(2,1)} %all_to_all.10) | data formatting | bytes 18874368 | tf_op jit(solution)/shard_map/reshape | solution.py:54
  546.7 8.7 %fusion.5 = f32[1152,384]{1,0:T(8,128)S(1)} fusion(bf16[1152,4096]{1,0:T(8,128)(2,1)} %reshape.115, bf16[1,4096,384]{2,1,0:T(8,128)(2,1)} %param.15), kind=kOutput, calls=%fused_computation.11 | convolution fusion | flops 3623878656 | bytes 14352384 | tf_op jit(solution)/shard_map/dot_general | solution.py:55
  555.4 6.2 fusion.7
  561.6 2.2 dot_general.17
  563.7 8.7 %convolution_convert_fusion = bf16[64,18,4096]{2,0,1:T(8,128)(2,1)} fusion(bf16[1,384,4096]{2,1,0:T(8,128)(2,1)S(1)} %copy-done, bf16[64,18,384]{2,1,0:T(8,128)(2,1)} %dot_general.17), kind=kOutput, calls=%fused_computation.3 | convolution fusion | flops 3628597248 | bytes 13467648 | tf_op jit(solution)/shard_map/dot_general | solution.py:58
  572.4 87.5 %reduce-scatter.2.cloned.1.call-done = bf16[64,18,1024]{2,0,1:T(8,128)(2,1)} async-done(((bf16[64,18,4096]{2,0,1:T(8,128)(2,1)}), bf16[64,18,1024]{2,0,1:T(8,128)(2,1)}) %reduce-scatter.2.cloned.1.call-update) | async-done | bytes 2359312 | tf_op jit(solution)/shard_map/reduce_scatter | solution.py:60
  660.0 4.7 copy.27
  664.7 10.9 %all-to-all-start.1 = ((bf16[64,18,1024]{2,1,0:T(8,128)(2,1)}), bf16[64,18,1024]{2,1,0:T(8,128)(2,1)}, u32[]{:S(2)}, u32[]{:S(2)}) async-start(bf16[64,18,1024]{2,1,0:T(8,128)(2,1)} %copy.27), calls=%async_computation.2 | async-start | bytes 6291456 | tf_op jit(solution)/shard_map/all_to_all | solution.py:63
  675.7 73.5 %all-to-all-done.1 = bf16[64,18,1024]{2,1,0:T(8,128)(2,1)} async-done(((bf16[64,18,1024]{2,1,0:T(8,128)(2,1)}), bf16[64,18,1024]{2,1,0:T(8,128)(2,1)}, u32[]{:S(2)}, u32[]{:S(2)}) %all-to-all-start.1) | async-done | bytes 2359328 | tf_op jit(solution)/shard_map/all_to_all | solution.py:63
  749.3 4.3 reshape.116
  753.6 8.0 %gather_fusion.1 = bf16[1024,1024]{1,0:T(8,128)(2,1)} fusion(bf16[1152,1024]{1,0:T(8,128)(2,1)} %reshape.116, s32[1024]{0:T(1024)S(1)} %broadcast_clamp_fusion), kind=kCustom, calls=%fused_computation.1 | custom fusion | bytes 4198400 | tf_op jit(solution)/shard_map/gather | solution.py:64
  761.6 2.9 fusion.2
  764.5 1.7 add_convert_fusion.1
  (41 shorter events, 5.5 us)
Async XLA Ops:
  6.5 557.2 %copy-start = (bf16[1,384,4096]{2,1,0:T(8,128)(2,1)S(1)}, bf16[1,384,4096]{2,1,0:T(8,128)(2,1)}, u32[]{:S(2)}) copy-start(bf16[1,384,4096]{2,1,0:T(8,128)(2,1)} %param.17) | copy-start | bytes 9437188
  6.5 88.3 %all-gather.4.cloned.1.call-start = ((), (), s32[]{:S(2)}) async-start(), calls=%async_computation.3 | async-start | bytes 8519680 | tf_op jit(solution)/shard_map/all_gather | solution.py:28
  7.3 95.3 %copy-start.3 = (s32[128,8]{0,1:T(8,128)S(1)}, s32[128,8]{0,1:T(8,128)}, u32[]{:S(2)}) copy-start(s32[128,8]{0,1:T(8,128)} %param.13) | copy-start | bytes 12292
  7.3 179.7 %all-gather.6.cloned.1.call-start = ((), (), s32[]{:S(2)}) async-start(), calls=%async_computation.5 | async-start | bytes 10485760 | tf_op jit(solution)/shard_map/all_gather | solution.py:31
  102.5 34.5 %copy-start.4 = (bf16[4096]{0:T(1024)(128)(2,1)S(1)}, bf16[4096]{0:T(1024)(128)(2,1)}, u32[]{:S(2)}) copy-start(bf16[4096]{0:T(1024)(128)(2,1)} %param.12) | copy-start | bytes 24580
  102.6 557.4 %reduce-scatter.2.cloned.1.call-start = ((), (), s32[]{:S(2)}) async-start(), calls=%async_computation.4 | async-start | bytes 11796480 | tf_op jit(solution)/shard_map/reduce_scatter | solution.py:60
  194.8 1.1 copy-start.2
  546.7 8.7 %copy-start.1 = (bf16[1152,4096]{1,0:T(8,128)(2,1)S(1)}, bf16[1152,4096]{1,0:T(8,128)(2,1)}, u32[]{:S(2)}) copy-start(bf16[1152,4096]{1,0:T(8,128)(2,1)} %reshape.115) | copy-start | bytes 28311556
  546.7 8.7 %copy-start.6 = (bf16[1,4096,384]{2,1,0:T(8,128)(2,1)S(1)}, bf16[1,4096,384]{2,1,0:T(8,128)(2,1)}, u32[]{:S(2)}) copy-start(bf16[1,4096,384]{2,1,0:T(8,128)(2,1)} %param.16) | copy-start | bytes 9437188
  664.7 10.9 %copy-start.5 = (f32[128,8]{0,1:T(8,128)S(1)}, f32[128,8]{0,1:T(8,128)}, u32[]{:S(2)}) copy-start(f32[128,8]{0,1:T(8,128)} %param.14) | copy-start | bytes 12292
  664.7 84.5 %all-to-all-start.1 = ((bf16[64,18,1024]{2,1,0:T(8,128)(2,1)}), bf16[64,18,1024]{2,1,0:T(8,128)(2,1)}, u32[]{:S(2)}, u32[]{:S(2)}) async-start(bf16[64,18,1024]{2,1,0:T(8,128)(2,1)} %copy.27), calls=%async_computation.2 | async-start | bytes 6291456 | tf_op jit(solution)/shard_map/all_to_all | solution.py:63
Sparse Core Ops, SparseCore 0:
  10.1 84.6 all-gather.3
  102.7 84.2 all-gather.5
  572.6 87.3 reduce-scatter.1
